TPU v7x, 32 devices: a whole 2x2x4 slice. The times are simulated.
32 devices in a mesh: row: 4 (over y, x), col: 8 (over z, core).
Axes of the slice: x: 2, y: 2, z: 4, core: 2. Of those that a mesh axis runs over, the one named last changes fastest.
Arguments:
- fact_block: int32 [98304, 1], P(('row', 'col')), may hold values from 0 to 31; in each aligned block of 3072 rows (0 to 3071, 3072 to 6143, ...) at most 192 rows name the same one
- fact_offset: int32 [98304], P(('row', 'col')), may hold values from 0 to 2047
- fact_date: int32 [98304], P(('row', 'col')), may hold values from 0 to 2555
- revenue: bfloat16 [98304], P(('row', 'col')), may hold values from 0.5 to 4
- supplier_words: int32 [2208], P('col'), may hold values from 0 to 1073741823
- date_words: int32 [88], P('col'), may hold values from 0 to 1073741823
- candidates: int32 [1024], replicated, may hold values from 0 to 65535
Outputs:
- supplier_revenue: float32 [65536], P(('row', 'col'))
- candidate_revenue: float32 [1024], replicated
- candidate_total: float32 [], replicated
Inputs may be any that keep to these rules, and one draw needn't show every extreme that they name: `fact_block`: each device's rows name no owner block more than 192 times. `candidates`: ids may repeat.
All inputs are finite; a program needn't handle non-finite values.
Results may differ from a plain program's by a relative error of at most 0.0003.
Values sent between devices are 32-bit elements; how exact they have to be, the bound alone decides.
A program may use at most 64 MiB of HBM per device.

v0:
```python
import jax
import jax.numpy as jnp
from jax import lax
from jax.sharding import PartitionSpec as P

SUP_DEV = 2048


def filtered_revenue(owner, fact_offset, fact_date, revenue, supplier_all, date_all):
    words_per_block = (SUP_DEV + 29) // 30
    word_index = owner * words_per_block + fact_offset // 30
    supplier_word = jnp.take(supplier_all, word_index)
    supplier_bit = jnp.bitwise_and(jnp.right_shift(supplier_word, fact_offset % 30), 1)
    date_slot = fact_date // 30
    positions = jnp.arange(date_all.shape[0], dtype=jnp.int32)
    date_word = jnp.sum(
        jnp.where(date_slot[:, None] == positions[None, :], date_all[None, :], 0), axis=1
    )
    date_bit = jnp.bitwise_and(jnp.right_shift(date_word, fact_date % 30), 1)
    return jnp.where(supplier_bit * date_bit == 1, revenue, jnp.zeros_like(revenue))


def per_device(fact_block, fact_offset, fact_date, revenue, supplier_words, date_words, candidates):
    devices = lax.axis_size("row") * lax.axis_size("col")
    supplier_all, date_all = (
        lax.all_gather(supplier_words, "col", axis=0, tiled=True),
        lax.all_gather(date_words, "col", axis=0, tiled=True),
    )
    owner = fact_block[:, 0]
    masked = filtered_revenue(owner, fact_offset, fact_date, revenue, supplier_all, date_all)
    row_count = fact_offset.shape[0]
    capacity = max(2, 2 * row_count // devices)
    row_ids = jnp.arange(row_count, dtype=jnp.int32)
    earlier = (owner[:, None] == owner[None, :]) & (row_ids[None, :] < row_ids[:, None])
    ranking = jnp.sum(earlier, axis=1, dtype=jnp.int32)
    slot_index = owner * capacity + ranking
    slot_revenue = (
        jnp.zeros((devices * capacity,), jnp.float32).at[slot_index].set(masked.astype(jnp.float32))
    )
    slot_offset = (
        jnp.zeros((devices * capacity,), jnp.float32)
        .at[slot_index]
        .set(fact_offset.astype(jnp.float32))
    )
    payload = jnp.stack((slot_revenue, slot_offset), axis=-1)
    payload = payload.reshape(lax.axis_size("row"), lax.axis_size("col"), 2 * capacity)
    arrived = lax.all_to_all(
        lax.all_to_all(payload, "row", split_axis=0, concat_axis=0, tiled=True),
        "col",
        split_axis=1,
        concat_axis=1,
        tiled=True,
    )
    arrived = arrived.reshape(-1, 2)
    owned = jax.ops.segment_sum(
        arrived[:, 0], arrived[:, 1].astype(jnp.int32), num_segments=SUP_DEV
    )
    global_id = owner * SUP_DEV + fact_offset
    onehot_cands = (global_id[:, None] == candidates[None, :]).astype(jnp.bfloat16)
    own_terms = jnp.dot(masked[None, :], onehot_cands, preferred_element_type=jnp.float32)[0]
    candidate_revenue = lax.psum(own_terms, ("row", "col"))
    candidate_total = jnp.sum(candidate_revenue)
    return (owned, candidate_revenue, candidate_total)


def solution(mesh):
    in_specs = (
        P(("row", "col"), None),
        P(("row", "col")),
        P(("row", "col")),
        P(("row", "col")),
        P("col"),
        P("col"),
        P(),
    )
    out_specs = (P(("row", "col")), P(), P())
    return jax.shard_map(
        per_device, mesh=mesh, in_specs=in_specs, out_specs=out_specs, check_vma=False
    )
```

profile of v0, /device:TPU:0, one launch (start us, length us, event | category | flops | bytes accessed | tf_op | source)
XLA Modules:
  0.0 186.6 jit_solution(15897103582751986480)
XLA Ops:
  0.6 1.2 dynamic-slice
  3.2 3.9 %convert_reduce_fusion = s32[3072]{0:T(1024)S(1)} fusion(s32[3072]{0:T(1024)} %bitcast.11), kind=kLoop, calls=%fused_computation.4 | loop fusion | flops 47182848 | bytes 24576 | tf_op jit(solution)/shard_map/reduce_sum | solution.py:35
  7.0 0.7 compare_select_fusion
  7.8 0.7 add_select_fusion.1
  8.5 0.8 multiply_add_fusion
  9.3 0.9 dynamic-update-slice.1
  10.2 0.9 dynamic-update-slice
  11.0 30.3 %all-reduce.2 = (s32[88]{0:T(128)S(1)}, s32[2208]{0:T(1024)S(1)}) all-reduce(s32[88]{0:T(128)S(1)} %dynamic-update-slice.1, s32[2208]{0:T(1024)S(1)} %dynamic-update-slice), channel_id=1, replica_groups=mesh['row'=4,'col'=8] {'col'}, use_global_device_ids=true, to_apply=%add.1 | all-reduce | flops 2296 | bytes 18368
  41.3 0.3 select_reduce_fusion
  41.6 0.0 copy-start
  41.6 0.0 copy-start.1
  41.6 0.0 copy-start.2
  41.6 0.0 copy-start.4
  41.6 17.4 %gather_fusion = s32[3072]{0:T(1024)S(1)} fusion(s32[2208]{0:T(1024)S(1)} %get-tuple-element.4, s32[3072]{0:T(1024)S(1)} %get-tuple-element.8), kind=kCustom, calls=%fused_computation | custom fusion | bytes 36864 | tf_op jit(solution)/shard_map/jit(_take)/gather | solution.py:12
  59.0 0.0 copy-done
  59.0 0.0 copy-done.1
  59.1 0.0 copy-done.2
  59.1 0.0 copy-done.4
  59.1 11.8 %scatter_custom_fusion = f32[6144]{0:T(1024)S(1)} fusion(s32[3072]{0:T(1024)S(1)} %bitcast.16, f32[3072]{0:T(1024)S(1)} %get-tuple-element.5, f32[]{:T(128)} %constant.30.clone.1), kind=kCustom, calls=%fused_computation.35 | custom fusion | bytes 24580 | tf_op jit(solution)/shard_map/scatter | solution.py:38
  70.9 11.8 %scatter_custom_fusion.1 = f32[6144]{0:T(1024)S(1)} fusion(s32[3072]{0:T(1024)S(1)} %bitcast.17, f32[3072]{0:T(1024)S(1)} %get-tuple-element.9, f32[]{:T(128)} %constant.30.clone.1), kind=kCustom, calls=%fused_computation.33 | custom fusion | bytes 24580 | tf_op jit(solution)/shard_map/scatter | solution.py:43
  82.8 0.0 copy-start.5
  82.8 1.1 copy.14
  83.9 2.7 %reshape.27 = f32[4,8,384]{2,1,0:T(8,128)} reshape(f32[6144,2]{1,0:T(8,128)S(1)} %copy.14) | data formatting | bytes 98304 | tf_op jit(solution)/shard_map/reshape | solution.py:46
  86.6 3.7 %all-to-all-start = ((f32[4,8,384]{2,1,0:T(8,128)}), f32[4,8,384]{2,1,0:T(8,128)S(1)}, u32[]{:S(2)}, u32[]{:S(2)}) async-start(f32[4,8,384]{2,1,0:T(8,128)} %reshape.27), calls=%async_computation | async-start | bytes 98304 | tf_op jit(solution)/shard_map/all_to_all | solution.py:48
  90.4 4.8 %all-to-all-done = f32[4,8,384]{2,1,0:T(8,128)S(1)} async-done(((f32[4,8,384]{2,1,0:T(8,128)}), f32[4,8,384]{2,1,0:T(8,128)S(1)}, u32[]{:S(2)}, u32[]{:S(2)}) %all-to-all-start) | async-done | bytes 49184 | tf_op jit(solution)/shard_map/all_to_all | solution.py:48
  95.1 0.6 copy.15
  95.8 3.3 %all-to-all-start.1 = ((f32[4,8,384]{2,0,1:T(4,128)}), f32[4,8,384]{2,0,1:T(4,128)S(1)}, u32[]{:S(2)}, u32[]{:S(2)}) async-start(f32[4,8,384]{2,0,1:T(4,128)} %copy.15), calls=%async_computation.1 | async-start | bytes 98304 | tf_op jit(solution)/shard_map/all_to_all | solution.py:47
  99.1 0.0 copy-done.5
  99.1 2.0 %fusion.1 = f32[1,1024]{1,0:T(1,128)S(1)} fusion(bf16[3072,1]{0,1:T(2,128)(2,1)S(1)} %reshape.72, s32[1024]{0:T(1024)S(1)} %copy-done.5, s32[3072]{0:T(1024)S(1)} %get-tuple-element.7), kind=kOutput, calls=%fused_computation.7 | convolution fusion | flops 9437184 | bytes 26624 | tf_op jit(solution)/shard_map/dot_general | solution.py:60
  101.1 39.8 %psum.7 = f32[1024]{0:T(1024)S(1)} all-reduce(f32[1024]{0:T(1024)S(1)} %bitcast.19), channel_id=1, replica_groups=mesh['row'=4,'col'=8] {'row','col'}, use_global_device_ids=true, to_apply=%region_5.6 | all-reduce | flops 1024 | bytes 8192 | tf_op jit(solution)/shard_map/psum | solution.py:61
  141.0 0.0 copy-start.3
  141.0 0.6 reduce_sum.32
  141.6 0.0 all-to-all-done.1
  141.6 3.2 %reshape.28 = f32[6144,2]{1,0:T(8,128)S(1)} reshape(f32[4,8,384]{2,1,0:T(8,128)S(1)} %copy.16) | data formatting | bytes 98304 | tf_op jit(solution)/shard_map/reshape | solution.py:54
  144.8 0.9 slice_reduce_fusion
  145.7 0.0 copy-done.3
  145.7 1.7 fusion.5
  147.4 39.3 %scatter_custom_fusion.2 = f32[2048]{0:T(1024)} fusion(s32[6144]{0:T(1024)S(1)} %fusion.5, f32[6144]{0:T(1024)S(1)} %slice_reduce_fusion, f32[]{:T(128)} %constant.30.clone.1), kind=kCustom, calls=%fused_computation.43 | custom fusion | flops 6144 | bytes 8196 | tf_op jit(solution)/shard_map/scatter-add | solution.py:55
  (6 shorter events, 0.1 us)
Async XLA Ops:
  41.6 17.5 %copy-start = (s32[3072,1]{0,1:T(1,128)S(1)}, s32[3072,1]{0,1:T(1,128)}, u32[]{:S(2)}) copy-start(s32[3072,1]{0,1:T(1,128)} %param.7) | copy-start | bytes 36868
  41.6 17.5 %copy-start.1 = (s32[3072]{0:T(1024)S(1)}, s32[3072]{0:T(1024)}, u32[]{:S(2)}) copy-start(s32[3072]{0:T(1024)} %param.9) | copy-start | bytes 36868
  41.6 17.5 %copy-start.2 = (s32[3072]{0:T(1024)S(1)}, s32[3072]{0:T(1024)}, u32[]{:S(2)}) copy-start(s32[3072]{0:T(1024)} %param.8) | copy-start | bytes 36868
  41.6 17.5 %copy-start.4 = (bf16[3072]{0:T(1024)(128)(2,1)S(1)}, bf16[3072]{0:T(1024)(128)(2,1)}, u32[]{:S(2)}) copy-start(bf16[3072]{0:T(1024)(128)(2,1)} %param.10) | copy-start | bytes 18436
  82.8 16.3 %copy-start.5 = (s32[1024]{0:T(1024)S(1)}, s32[1024]{0:T(1024)}, u32[]{:S(2)}) copy-start(s32[1024]{0:T(1024)} %param.13) | copy-start | bytes 12292
  86.6 8.5 %all-to-all-start = ((f32[4,8,384]{2,1,0:T(8,128)}), f32[4,8,384]{2,1,0:T(8,128)S(1)}, u32[]{:S(2)}, u32[]{:S(2)}) async-start(f32[4,8,384]{2,1,0:T(8,128)} %reshape.27), calls=%async_computation | async-start | bytes 98304 | tf_op jit(solution)/shard_map/all_to_all | solution.py:48
  95.8 45.8 %all-to-all-start.1 = ((f32[4,8,384]{2,0,1:T(4,128)}), f32[4,8,384]{2,0,1:T(4,128)S(1)}, u32[]{:S(2)}, u32[]{:S(2)}) async-start(f32[4,8,384]{2,0,1:T(4,128)} %copy.15), calls=%async_computation.1 | async-start | bytes 98304 | tf_op jit(solution)/shard_map/all_to_all | solution.py:47
  141.0 4.7 %copy-start.3 = (f32[1024]{0:T(1024)}, f32[1024]{0:T(1024)S(1)}, u32[]{:S(2)}) copy-start(f32[1024]{0:T(1024)S(1)} %psum.7) | copy-start | bytes 12292
where the time goes:
time: 188 us; the launch traced here: 187 us
  blocking collectives  70.1 us (37%)
  local copies, waits for them, and re-layouts  52.5 us (28%)
  other arithmetic  48 us (26%)
  starting transfers between devices  7.06 us (4%)
  waiting for transfers between devices  4.79 us (3%)
  between operations  2.12 us (1%)
  matrix products  2.01 us (1%)
    psum x1, blocking collectives, per_device(): candidate_revenue = lax.psum(own_terms, ('row', 'col'))  39.8 us
    scatter-add x1, other arithmetic, per_device(): jax.ops.segment_sum(arrived[:, 0], arrived[:, 1].astype(jnp.int32), num_s...  39.3 us
    unnamed x1, blocking collectives  30.3 us
    gather x1, local copies, waits for them, and re-layouts, filtered_revenue(): supplier_word = jnp.take(supplier_all, word_index)  17.4 us
    scatter x1, local copies, waits for them, and re-layouts, per_device(): slot_offset = jnp.zeros((devices * capacity,), jnp.float32).at[slot_index...  11.8 us
    scatter x1, local copies, waits for them, and re-layouts, per_device(): jnp.zeros((devices * capacity,), jnp.float32).at[slot_index]  11.8 us
    all_to_all x1, waiting for transfers between devices, per_device(): lax.all_to_all(payload, 'row', split_axis=0, concat_axis=0, tiled=True)  4.79 us
    reduce_sum x1, other arithmetic, per_device(): ranking = jnp.sum(earlier, axis=1, dtype=jnp.int32)  3.86 us
  transfers between devices with their start and end apart: 2, of which 1 were waited for; matrix products, arithmetic and copies ran while one was open for 1% of the time, Pallas kernels for 0%

commit v1 on v0

v1 whole, which is shorter than its diff:
```python
import functools

import jax
import jax.numpy as jnp
from jax import lax
from jax.experimental import pallas as pl
from jax.experimental.pallas import tpu as pltpu
from jax.sharding import PartitionSpec as P

SUP_DEV = 2048
LANES = 128
WIDE = 2 * LANES
GROUP = SUP_DEV // WIDE
BITS = 30
MESH = pl.DeviceIdType.MESH


def div_bits(x):
    return lax.shift_right_logical(x * 2185, 16)


def lookup(row, index):
    table = jnp.broadcast_to(row, index.shape)
    return jnp.take_along_axis(table, index, axis=1, mode="promise_in_bounds")


def kernel(
    rows_axis, cols_axis, date_words,
    block_ref, offset_ref, date_ref, rev_ref, cand_ref, sup_ref, dat_ref,
    owned_ref, cand_out_ref, total_ref,
    a_idx, b_idx, left, right, hist, dat_buf, sup_buf, part1, sum1, part2,
    cpart, cpart1, csum1, cpart2,
    dat_send, dat_recv, sup_send, sup_recv, h1_send, h1_recv, c1_send, c1_recv,
    h2_send, h2_recv, c2_send, c2_recv,
):
    R, C = rows_axis, cols_axis
    i, j = lax.axis_index("row"), lax.axis_index("col")
    row_peers = [(lax.rem(i + k, R), j) for k in range(1, R)]
    col_peers = [(i, lax.rem(j + k, C)) for k in range(1, C)]
    n_rows = block_ref.shape[0]
    chunks = hist.shape[0] // left.shape[0]
    tall = left.shape[0]

    barrier = pltpu.get_barrier_semaphore()
    for peer in col_peers + row_peers:
        pl.semaphore_signal(barrier, inc=1, device_id=peer, device_id_type=MESH)

    off = offset_ref[...]
    a_idx[...] = block_ref[...] * GROUP + (lax.shift_right_logical(off, 7) & (GROUP - 1))
    b_idx[...] = lax.shift_right_logical(off, 10) * LANES + (off & (LANES - 1))

    pl.semaphore_wait(barrier, (C - 1) + (R - 1))

    def remote(src, dst, send, recv, peer):
        return pltpu.make_async_remote_copy(
            src_ref=src, dst_ref=dst, send_sem=send, recv_sem=recv, device_id=peer, device_id_type=MESH
        )

    dat_copies = [
        remote(dat_ref, dat_buf.at[k], dat_send.at[k], dat_recv.at[k], col_peers[k]) for k in range(C - 1)
    ]
    sup_copies = [
        remote(sup_ref, sup_buf.at[k + 1], sup_send.at[k], sup_recv.at[k], col_peers[k]) for k in range(C - 1)
    ]
    for copy in dat_copies:
        copy.start()
    for copy in sup_copies:
        copy.start()

    iota_b = lax.broadcasted_iota(jnp.int32, (WIDE, LANES), 0)
    for r in range(n_rows):
        hit = iota_b == b_idx[r : r + 1, :]
        right[:, r * LANES : (r + 1) * LANES] = jnp.where(hit, 1.0, 0.0).astype(jnp.bfloat16)

    iota_a = lax.broadcasted_iota(jnp.int32, (tall, LANES), 0)
    rev = rev_ref[...].astype(jnp.float32)

    def build_left(base, values):
        for r in range(n_rows):
            hit = iota_a == a_idx[r : r + 1, :] - base
            left[:, r * LANES : (r + 1) * LANES] = jnp.where(hit, values[r : r + 1, :], 0.0).astype(jnp.bfloat16)

    day = date_ref[...]
    day_word = div_bits(day)
    day_bit = day - day_word * BITS

    for copy in dat_copies:
        copy.wait_recv()
    table = pltpu.roll(dat_ref[...], j * date_words, 1)
    for k in range(1, C):
        source = lax.rem(j - k + C, C)
        table = table + pltpu.roll(dat_buf[k - 1], source * date_words, 1)
    lit = lax.shift_right_logical(lookup(table, day_word), day_bit) & 1
    values = jnp.where(lit == 1, rev, 0.0)

    def histogram(base):
        build_left(base, values)
        return lax.dot_general(
            left[...], right[...], (((1,), (1,)), ((), ())), preferred_element_type=jnp.float32
        )

    if chunks == 1:
        hist[...] = histogram(0)
    else:

        def body(c, carry):
            base = pl.multiple_of(c * tall, tall)
            hist[pl.ds(base, tall), :] = histogram(base)
            return carry

        lax.fori_loop(0, chunks, body, 0)

    span = C * GROUP
    h1_copies = [
        remote(
            hist.at[pl.ds(pl.multiple_of(row_peers[k][0] * span, span), span), :],
            part1.at[k], h1_send.at[k], h1_recv.at[k], row_peers[k],
        )
        for k in range(R - 1)
    ]
    for copy in h1_copies:
        copy.start()

    cand = cand_ref[...]
    c_off = cand & (SUP_DEV - 1)
    c_owner = lax.div(cand, SUP_DEV) if SUP_DEV & (SUP_DEV - 1) else lax.shift_right_logical(cand, 11)
    c_row = c_owner * GROUP + (lax.shift_right_logical(c_off, 7) & (GROUP - 1))
    c_high = c_off >= SUP_DEV // 2
    c_lane = c_off & (LANES - 1)

    def pick(g, acc):
        base = pl.multiple_of(g * 8, 8)
        tile = hist[pl.ds(base, 8), :]
        for s in range(8):
            low = lookup(tile[s : s + 1, :LANES], c_lane)
            high = lookup(tile[s : s + 1, LANES:], c_lane)
            acc = jnp.where(c_row == base + s, jnp.where(c_high, high, low), acc)
        return acc

    picked = lax.fori_loop(0, hist.shape[0] // 8, pick, jnp.zeros(cand.shape, jnp.float32))
    cpart[...] = picked
    cpart1[i] = picked
    c1_copies = [
        remote(cpart, cpart1.at[i], c1_send.at[k], c1_recv.at[k], row_peers[k]) for k in range(R - 1)
    ]
    for copy in c1_copies:
        copy.start()

    sup_buf[0] = sup_ref[...]
    for copy in sup_copies:
        copy.wait_recv()
    c_word = div_bits(c_off)
    c_bit = c_off - c_word * BITS

    def word_of(k, acc):
        source = lax.rem(j - k + C, C)
        for r in range(R):
            word = lookup(sup_buf[k, r : r + 1, :], c_word)
            acc = jnp.where(c_owner == source * R + r, word, acc)
        return acc

    c_words = lax.fori_loop(0, C, word_of, jnp.zeros(cand.shape, jnp.int32))
    c_lit = (lax.shift_right_logical(c_words, c_bit) & 1) == 1

    me = i * C + j
    holder = me // R
    slot = lax.rem(j - holder + C, C)
    my_words = sup_buf[slot, pl.ds(lax.rem(me, R), 1), :]
    spot = lax.broadcasted_iota(jnp.int32, owned_ref.shape, 0) * LANES + lax.broadcasted_iota(
        jnp.int32, owned_ref.shape, 1
    )
    spot_word = div_bits(spot)
    my_lit = (lax.shift_right_logical(lookup(my_words, spot_word), spot - spot_word * BITS) & 1) == 1

    for copy in h1_copies:
        copy.wait_recv()
    total = hist[pl.ds(pl.multiple_of(i * span, span), span), :]
    for k in range(R - 1):
        total = total + part1[k]
    sum1[...] = total
    h2_copies = [
        remote(
            sum1.at[pl.ds(pl.multiple_of(col_peers[k][1] * GROUP, GROUP), GROUP), :],
            part2.at[k], h2_send.at[k], h2_recv.at[k], col_peers[k],
        )
        for k in range(C - 1)
    ]
    for copy in h2_copies:
        copy.start()
    for copy in c1_copies:
        copy.wait_recv()
    ctotal = cpart1[0]
    for k in range(1, R):
        ctotal = ctotal + cpart1[k]
    csum1[...] = ctotal
    cpart2[j] = ctotal
    c2_copies = [
        remote(csum1, cpart2.at[j], c2_send.at[k], c2_recv.at[k], col_peers[k]) for k in range(C - 1)
    ]
    for copy in c2_copies:
        copy.start()

    for copy in h2_copies:
        copy.wait_recv()
    mine = sum1[pl.ds(pl.multiple_of(j * GROUP, GROUP), GROUP), :]
    for k in range(C - 1):
        mine = mine + part2[k]
    owned_ref[:GROUP, :] = jnp.where(my_lit[:GROUP], mine[:, :LANES], 0.0)
    owned_ref[GROUP:, :] = jnp.where(my_lit[GROUP:], mine[:, LANES:], 0.0)

    for copy in c2_copies:
        copy.wait_recv()
    ctotal = cpart2[0]
    for k in range(1, C):
        ctotal = ctotal + cpart2[k]
    result = jnp.where(c_lit, ctotal, 0.0)
    cand_out_ref[...] = result
    total_ref[0, 0] = jnp.sum(result)

    for copy in dat_copies + sup_copies + h1_copies + c1_copies + h2_copies + c2_copies:
        copy.wait_send()


def per_device(R, C, fact_block, fact_offset, fact_date, revenue, supplier_words, date_words, candidates):
    rows = fact_offset.shape[0] // LANES
    cands = candidates.shape[0] // LANES
    n_dates = date_words.shape[0]
    per_block = supplier_words.shape[0] // R
    tall_all = R * C * GROUP
    tall = min(tall_all, WIDE)
    words = jnp.pad(supplier_words.reshape(R, per_block), ((0, 0), (0, LANES - per_block)))
    dates = jnp.pad(date_words.reshape(1, n_dates), ((0, 0), (0, LANES - n_dates)))
    span = C * GROUP
    f32, i32 = jnp.float32, jnp.int32
    dma = pltpu.SemaphoreType.DMA
    vmem = pl.BlockSpec(memory_space=pltpu.VMEM)
    owned, cand_rev, total = pl.pallas_call(
        functools.partial(kernel, R, C, n_dates),
        out_shape=(
            jax.ShapeDtypeStruct((SUP_DEV // LANES, LANES), f32),
            jax.ShapeDtypeStruct((cands, LANES), f32),
            jax.ShapeDtypeStruct((1, 1), f32),
        ),
        in_specs=[vmem] * 7,
        out_specs=(vmem, vmem, pl.BlockSpec(memory_space=pltpu.SMEM)),
        scratch_shapes=[
            pltpu.VMEM((rows, LANES), i32),
            pltpu.VMEM((rows, LANES), i32),
            pltpu.VMEM((tall, rows * LANES), jnp.bfloat16),
            pltpu.VMEM((WIDE, rows * LANES), jnp.bfloat16),
            pltpu.VMEM((tall_all, WIDE), f32),
            pltpu.VMEM((C - 1, 1, LANES), i32),
            pltpu.VMEM((C, R, LANES), i32),
            pltpu.VMEM((R - 1, span, WIDE), f32),
            pltpu.VMEM((span, WIDE), f32),
            pltpu.VMEM((C - 1, GROUP, WIDE), f32),
            pltpu.VMEM((cands, LANES), f32),
            pltpu.VMEM((R, cands, LANES), f32),
            pltpu.VMEM((cands, LANES), f32),
            pltpu.VMEM((C, cands, LANES), f32),
            dma((C - 1,)), dma((C - 1,)), dma((C - 1,)), dma((C - 1,)),
            dma((R - 1,)), dma((R - 1,)), dma((R - 1,)), dma((R - 1,)),
            dma((C - 1,)), dma((C - 1,)), dma((C - 1,)), dma((C - 1,)),
        ],
        compiler_params=pltpu.CompilerParams(collective_id=0, has_side_effects=True),
        name="revenue",
    )(
        fact_block.reshape(rows, LANES),
        fact_offset.reshape(rows, LANES),
        fact_date.reshape(rows, LANES),
        revenue.reshape(rows, LANES),
        candidates.reshape(cands, LANES),
        words,
        dates,
    )
    return owned.reshape(SUP_DEV), cand_rev.reshape(candidates.shape), total.reshape(())


def solution(mesh):
    in_specs = (
        P(("row", "col"), None),
        P(("row", "col")),
        P(("row", "col")),
        P(("row", "col")),
        P("col"),
        P("col"),
        P(),
    )
    out_specs = (P(("row", "col")), P(), P())
    body = functools.partial(per_device, mesh.shape["row"], mesh.shape["col"])
    return jax.shard_map(body, mesh=mesh, in_specs=in_specs, out_specs=out_specs, check_vma=False)
```

time: 188 us -> 28.5 us (0.15)
  blocking collectives: 70.1 us -> 0 us
  local copies, waits for them, and re-layouts: 52.5 us -> 3.79 us
  other arithmetic: 48 us -> 0 us
  Pallas kernels: 0 us -> 21.9 us
  starting transfers between devices: 7.06 us -> 0 us
  waiting for transfers between devices: 4.79 us -> 0 us
  matrix products: 2.01 us -> 0 us
    psum x1 -> x0, blocking collectives: 39.8 us -> none  [per_device(): candidate_revenue = lax.psum(own_terms, ('row', 'col'))]
    scatter-add x1 -> x0, other arithmetic: 39.3 us -> none  [per_device(): jax.ops.segment_sum(arrived[:, 0], arrived[:, 1].astype(jnp.int32), num_s...]
    unnamed x1 -> x0, blocking collectives: 30.3 us -> none
    scatter x2 -> x0, local copies, waits for them, and re-layouts: 23.6 us -> none  [the longest x1 11.8 us: per_device(): slot_offset = jnp.zeros((devices * capacity,), jnp.float32).at[slot_index...]
    pallas_call x0 -> x1, Pallas kernels: none -> 21.9 us  [per_device(): pl.pallas_call(functools.partial(kernel, R, C, n_dates), out_shape=(jax.S...]
    gather x1 -> x0, local copies, waits for them, and re-layouts: 17.4 us -> none  [filtered_revenue(): supplier_word = jnp.take(supplier_all, word_index)]
    all_to_all x2 -> x0, starting transfers between devices: 7.06 us -> none  [the longest x1 3.72 us: per_device(): lax.all_to_all(payload, 'row', split_axis=0, concat_axis=0, tiled=True)]
    reshape x2 -> x1, local copies, waits for them, and re-layouts: 5.9 us -> 0.08 us  [per_device(): supplier_words.reshape(R, per_block)]
  transfers between devices with their start and end apart: 2 -> 0, of which waited for: 1 -> 0; matrix products, arithmetic and copies ran while one was open for 1% -> 0% of each run, Pallas kernels for 0% -> 0%
where the time goes in v1:
time: 28.5 us; the launch traced here: 28.2 us
  Pallas kernels  21.9 us (77%)
  local copies, waits for them, and re-layouts  3.79 us (13%)
  between operations  2.49 us (9%)
    pallas_call x1, Pallas kernels, per_device(): pl.pallas_call(functools.partial(kernel, R, C, n_dates), out_shape=(jax.S...  21.9 us
    unnamed x10, local copies, waits for them, and re-layouts  2.61 us
    pad x1, local copies, waits for them, and re-layouts, per_device(): jnp.pad(supplier_words.reshape(R, per_block), ((0, 0), (0, LANES - per_bl...  0.59 us

profile of v1, /device:TPU:0, one launch (start us, length us, event | category | flops | bytes accessed | tf_op | source)
XLA Modules:
  0.0 28.2 jit_solution(18289546926989219800)
XLA Ops:
  0.6 0.0 copy-start.3
  0.6 0.0 copy-start.2
  0.7 0.6 %copy-done.3 = s32[11]{0:T(128)S(1)} copy-done((s32[11]{0:T(128)S(1)}, s32[11]{0:T(128)}, u32[]{:S(2)}) %copy-start.3) | copy-done | bytes 68
  1.3 0.5 %pad.9.dat_ref = s32[1,128]{1,0:T(1,128)} pad(s32[1,11]{1,0:T(1,128)S(1)} %bitcast.16, s32[]{:T(128)} %constant.0.clone.1), padding=0_0x0_117 | pad | bytes 560 | tf_op jit(solution)/shard_map/jit(_pad)/pad | solution.py:232
  1.8 0.0 copy-done.2
  1.8 0.1 reshape.41
  1.9 0.6 %pad.8.sup_ref = s32[4,128]{1,0:T(4,128)} pad(s32[4,69]{1,0:T(4,128)S(1)} %reshape.41, s32[]{:T(128)} %constant.0.clone.1), padding=0_0x0_59 | pad | bytes 3156 | tf_op jit(solution)/shard_map/jit(_pad)/pad | solution.py:231
  2.5 21.9 %revenue.1 = (f32[16,128]{1,0:T(8,128)}, f32[8,128]{1,0:T(8,128)}, f32[1,1]{1,0:T(1,128)}) custom-call(s32[24,128]{1,0:T(8,128)} %bitcast.9, s32[24,128]{1,0:T(8,128)} %bitcast.10, s32[24,128]{1,0:T(8,128)} %bitcast.11, bf16[24,128]{1,0:T(8,128)(2,1)} %bitcast.13, s32[8,128]{1,0:T(8,128)} %bitcast.14, s32[4,128]{1,0:T(4,128)} %pad.8.sup_ref, ...), custom_call_target="tpu_custom_call" | custom-call | tf_op jit(solution)/shard_map/revenue/pallas_call | solution.py:237
  24.4 0.0 copy-start
  24.4 0.7 %copy-done = f32[16,128]{1,0:T(8,128)S(1)} copy-done((f32[16,128]{1,0:T(8,128)S(1)}, f32[16,128]{1,0:T(8,128)}, u32[]{:S(2)}) %copy-start) | copy-done | bytes 8216
  25.1 0.0 copy-start.1
  25.1 0.6 %copy.13 = f32[2048]{0:T(1024)} copy(f32[2048]{0:T(1024)S(1)} %bitcast.12) | data formatting | bytes 16384
  25.7 0.1 copy-done.1
  25.8 0.6 %copy.14 = f32[1024]{0:T(1024)} copy(f32[1024]{0:T(1024)S(1)} %bitcast.15) | data formatting | bytes 8192
Async XLA Ops:
  0.6 0.7 %copy-start.3 = (s32[11]{0:T(128)S(1)}, s32[11]{0:T(128)}, u32[]{:S(2)}) copy-start(s32[11]{0:T(128)} %param.12) | copy-start | bytes 136
  0.6 1.2 %copy-start.2 = (s32[276]{0:T(512)S(1)}, s32[276]{0:T(512)}, u32[]{:S(2)}) copy-start(s32[276]{0:T(512)} %param.11) | copy-start | bytes 3316
  24.4 0.7 %copy-start = (f32[16,128]{1,0:T(8,128)S(1)}, f32[16,128]{1,0:T(8,128)}, u32[]{:S(2)}) copy-start(f32[16,128]{1,0:T(8,128)} %get-tuple-element.6) | copy-start | bytes 24580
  25.1 0.7 %copy-start.1 = (f32[8,128]{1,0:T(8,128)S(1)}, f32[8,128]{1,0:T(8,128)}, u32[]{:S(2)}) copy-start(f32[8,128]{1,0:T(8,128)} %get-tuple-element.7) | copy-start | bytes 12292

commit v2 on v1

--- a/solution.py
+++ b/solution.py
@@ -25,9 +25,10 @@
 
 
 def kernel(
-    rows_axis, cols_axis, date_words,
-    block_ref, offset_ref, date_ref, rev_ref, cand_ref, sup_ref, dat_ref,
-    owned_ref, cand_out_ref, total_ref,
+    rows_axis, cols_axis,
+    block_in, offset_in, date_in, rev_in, cand_in, sup_in, dat_in,
+    both_ref, total_ref,
+    block_ref, offset_ref, date_ref, rev_ref, cand_ref, load_sem, dat_row,
     a_idx, b_idx, left, right, hist, dat_buf, sup_buf, part1, sum1, part2,
     cpart, cpart1, csum1, cpart2,
     dat_send, dat_recv, sup_send, sup_recv, h1_send, h1_recv, c1_send, c1_recv,
@@ -38,12 +39,26 @@
     row_peers = [(lax.rem(i + k, R), j) for k in range(1, R)]
     col_peers = [(i, lax.rem(j + k, C)) for k in range(1, C)]
     n_rows = block_ref.shape[0]
+    n_dates, n_words = dat_in.shape[1], sup_in.shape[0]
+    per_block = n_words // R
+    owned_rows = both_ref.shape[0] - cand_ref.shape[0]
     chunks = hist.shape[0] // left.shape[0]
     tall = left.shape[0]
 
     barrier = pltpu.get_barrier_semaphore()
     for peer in col_peers + row_peers:
         pl.semaphore_signal(barrier, inc=1, device_id=peer, device_id_type=MESH)
+
+    pairs = [
+        (offset_in, offset_ref), (block_in, block_ref), (date_in, date_ref), (rev_in, rev_ref),
+        (cand_in, cand_ref), (dat_in, dat_buf.at[j]), (sup_in, sup_buf.at[j, 0]),
+    ]
+    loads = [pltpu.make_async_copy(src, dst, load_sem.at[n]) for n, (src, dst) in enumerate(pairs)]
+    for load in loads:
+        load.start()
+    dat_row[...] = jnp.zeros_like(dat_row)
+    for load in loads:
+        load.wait()
 
     off = offset_ref[...]
     a_idx[...] = block_ref[...] * GROUP + (lax.shift_right_logical(off, 7) & (GROUP - 1))
@@ -57,10 +72,10 @@
         )
 
     dat_copies = [
-        remote(dat_ref, dat_buf.at[k], dat_send.at[k], dat_recv.at[k], col_peers[k]) for k in range(C - 1)
+        remote(dat_in, dat_buf.at[j], dat_send.at[k], dat_recv.at[k], col_peers[k]) for k in range(C - 1)
     ]
     sup_copies = [
-        remote(sup_ref, sup_buf.at[k + 1], sup_send.at[k], sup_recv.at[k], col_peers[k]) for k in range(C - 1)
+        remote(sup_in, sup_buf.at[j, 0], sup_send.at[k], sup_recv.at[k], col_peers[k]) for k in range(C - 1)
     ]
     for copy in dat_copies:
         copy.start()
@@ -86,10 +101,9 @@
 
     for copy in dat_copies:
         copy.wait_recv()
-    table = pltpu.roll(dat_ref[...], j * date_words, 1)
-    for k in range(1, C):
-        source = lax.rem(j - k + C, C)
-        table = table + pltpu.roll(dat_buf[k - 1], source * date_words, 1)
+    for c in range(C):
+        dat_row[:, c * n_dates : (c + 1) * n_dates] = dat_buf[c]
+    table = dat_row[...]
     lit = lax.shift_right_logical(lookup(table, day_word), day_bit) & 1
     values = jnp.where(lit == 1, rev, 0.0)
 
@@ -146,31 +160,35 @@
     for copy in c1_copies:
         copy.start()
 
-    sup_buf[0] = sup_ref[...]
     for copy in sup_copies:
         copy.wait_recv()
+
+    full = n_words // LANES
+
+    def words_at(source, flat):
+        word = lookup(sup_buf[source, :, n_words - LANES :], jnp.maximum(flat - (n_words - LANES), 0))
+        for t in range(full):
+            near = (flat >= t * LANES) & (flat < (t + 1) * LANES)
+            word = jnp.where(near, lookup(sup_buf[source, :, t * LANES : (t + 1) * LANES], flat & (LANES - 1)), word)
+        return word
+
     c_word = div_bits(c_off)
     c_bit = c_off - c_word * BITS
-
-    def word_of(k, acc):
-        source = lax.rem(j - k + C, C)
-        for r in range(R):
-            word = lookup(sup_buf[k, r : r + 1, :], c_word)
-            acc = jnp.where(c_owner == source * R + r, word, acc)
-        return acc
+    c_col = lax.div(c_owner, R)
+    c_flat = (c_owner - c_col * R) * per_block + c_word
+
+    def word_of(source, acc):
+        return jnp.where(c_col == source, words_at(source, c_flat), acc)
 
     c_words = lax.fori_loop(0, C, word_of, jnp.zeros(cand.shape, jnp.int32))
     c_lit = (lax.shift_right_logical(c_words, c_bit) & 1) == 1
 
     me = i * C + j
-    holder = me // R
-    slot = lax.rem(j - holder + C, C)
-    my_words = sup_buf[slot, pl.ds(lax.rem(me, R), 1), :]
-    spot = lax.broadcasted_iota(jnp.int32, owned_ref.shape, 0) * LANES + lax.broadcasted_iota(
-        jnp.int32, owned_ref.shape, 1
-    )
+    shape = (owned_rows, LANES)
+    spot = lax.broadcasted_iota(jnp.int32, shape, 0) * LANES + lax.broadcasted_iota(jnp.int32, shape, 1)
     spot_word = div_bits(spot)
-    my_lit = (lax.shift_right_logical(lookup(my_words, spot_word), spot - spot_word * BITS) & 1) == 1
+    my_words = words_at(me // R, lax.rem(me, R) * per_block + spot_word)
+    my_lit = (lax.shift_right_logical(my_words, spot - spot_word * BITS) & 1) == 1
 
     for copy in h1_copies:
         copy.wait_recv()
@@ -205,8 +223,8 @@
     mine = sum1[pl.ds(pl.multiple_of(j * GROUP, GROUP), GROUP), :]
     for k in range(C - 1):
         mine = mine + part2[k]
-    owned_ref[:GROUP, :] = jnp.where(my_lit[:GROUP], mine[:, :LANES], 0.0)
-    owned_ref[GROUP:, :] = jnp.where(my_lit[GROUP:], mine[:, LANES:], 0.0)
+    both_ref[:GROUP, :] = jnp.where(my_lit[:GROUP], mine[:, :LANES], 0.0)
+    both_ref[GROUP:owned_rows, :] = jnp.where(my_lit[GROUP:], mine[:, LANES:], 0.0)
 
     for copy in c2_copies:
         copy.wait_recv()
@@ -214,7 +232,7 @@
     for k in range(1, C):
         ctotal = ctotal + cpart2[k]
     result = jnp.where(c_lit, ctotal, 0.0)
-    cand_out_ref[...] = result
+    both_ref[owned_rows:, :] = result
     total_ref[0, 0] = jnp.sum(result)
 
     for copy in dat_copies + sup_copies + h1_copies + c1_copies + h2_copies + c2_copies:
@@ -224,33 +242,35 @@
 def per_device(R, C, fact_block, fact_offset, fact_date, revenue, supplier_words, date_words, candidates):
     rows = fact_offset.shape[0] // LANES
     cands = candidates.shape[0] // LANES
-    n_dates = date_words.shape[0]
-    per_block = supplier_words.shape[0] // R
     tall_all = R * C * GROUP
     tall = min(tall_all, WIDE)
-    words = jnp.pad(supplier_words.reshape(R, per_block), ((0, 0), (0, LANES - per_block)))
-    dates = jnp.pad(date_words.reshape(1, n_dates), ((0, 0), (0, LANES - n_dates)))
     span = C * GROUP
     f32, i32 = jnp.float32, jnp.int32
     dma = pltpu.SemaphoreType.DMA
     vmem = pl.BlockSpec(memory_space=pltpu.VMEM)
-    owned, cand_rev, total = pl.pallas_call(
-        functools.partial(kernel, R, C, n_dates),
+    both, total = pl.pallas_call(
+        functools.partial(kernel, R, C),
         out_shape=(
-            jax.ShapeDtypeStruct((SUP_DEV // LANES, LANES), f32),
-            jax.ShapeDtypeStruct((cands, LANES), f32),
+            jax.ShapeDtypeStruct((SUP_DEV // LANES + cands, LANES), f32),
             jax.ShapeDtypeStruct((1, 1), f32),
         ),
-        in_specs=[vmem] * 7,
-        out_specs=(vmem, vmem, pl.BlockSpec(memory_space=pltpu.SMEM)),
+        in_specs=[pl.BlockSpec(memory_space=pl.ANY)] * 7,
+        out_specs=(vmem, pl.BlockSpec(memory_space=pltpu.SMEM)),
         scratch_shapes=[
+            pltpu.VMEM((rows, LANES), i32),
+            pltpu.VMEM((rows, LANES), i32),
+            pltpu.VMEM((rows, LANES), i32),
+            pltpu.VMEM((rows, LANES), revenue.dtype),
+            pltpu.VMEM((cands, LANES), i32),
+            dma((7,)),
+            pltpu.VMEM((1, LANES), i32),
             pltpu.VMEM((rows, LANES), i32),
             pltpu.VMEM((rows, LANES), i32),
             pltpu.VMEM((tall, rows * LANES), jnp.bfloat16),
             pltpu.VMEM((WIDE, rows * LANES), jnp.bfloat16),
             pltpu.VMEM((tall_all, WIDE), f32),
-            pltpu.VMEM((C - 1, 1, LANES), i32),
-            pltpu.VMEM((C, R, LANES), i32),
+            pltpu.VMEM((C, 1, date_words.shape[0]), i32),
+            pltpu.VMEM((C, 1, supplier_words.shape[0]), i32),
             pltpu.VMEM((R - 1, span, WIDE), f32),
             pltpu.VMEM((span, WIDE), f32),
             pltpu.VMEM((C - 1, GROUP, WIDE), f32),
@@ -270,10 +290,11 @@
         fact_date.reshape(rows, LANES),
         revenue.reshape(rows, LANES),
         candidates.reshape(cands, LANES),
-        words,
-        dates,
+        supplier_words,
+        date_words.reshape(1, -1),
     )
-    return owned.reshape(SUP_DEV), cand_rev.reshape(candidates.shape), total.reshape(())
+    owned = both[: SUP_DEV // LANES].reshape(SUP_DEV)
+    return owned, both[SUP_DEV // LANES :].reshape(candidates.shape), total.reshape(())
 
 
 def solution(mesh):

time: 28.5 us -> 26.1 us (0.916)
  local copies, waits for them, and re-layouts: 3.79 us -> 1.94 us
  Pallas kernels: 21.9 us -> 21.5 us
    unnamed x10 -> x2, local copies, waits for them, and re-layouts: 2.61 us -> 0.01 us
    reshape x1 -> x2, local copies, waits for them, and re-layouts: 0.08 us -> 1.94 us  [the longest x1 1.34 us: per_device(): both[SUP_DEV // LANES:].reshape(candidates.shape)]
    pad x2 -> x0, local copies, waits for them, and re-layouts: 1.1 us -> none  [the longest x1 0.59 us: per_device(): jnp.pad(supplier_words.reshape(R, per_block), ((0, 0), (0, LANES - per_bl...]
    pallas_call x1, Pallas kernels: 21.9 us -> 21.5 us  [per_device(): pl.pallas_call(functools.partial(kernel, R, C), out_shape=(jax.ShapeDtype...]
where the time goes in v2:
time: 26.1 us; the launch traced here: 25.9 us
  Pallas kernels  21.5 us (82%)
  between operations  2.41 us (9%)
  local copies, waits for them, and re-layouts  1.94 us (7%)
    pallas_call x1, Pallas kernels, per_device(): pl.pallas_call(functools.partial(kernel, R, C), out_shape=(jax.ShapeDtype...  21.5 us
    reshape x1, local copies, waits for them, and re-layouts, per_device(): both[SUP_DEV // LANES:].reshape(candidates.shape)  1.34 us
    reshape x1, local copies, waits for them, and re-layouts, per_device(): owned = both[:SUP_DEV // LANES].reshape(SUP_DEV)  0.6 us

profile of v2, /device:TPU:0, one launch (start us, length us, event | category | flops | bytes accessed | tf_op | source)
XLA Modules:
  0.0 25.9 jit_solution(8013339895185738005)
XLA Ops:
  0.6 21.5 %revenue.1 = (f32[24,128]{1,0:T(8,128)}, f32[1,1]{1,0:T(1,128)}) custom-call(s32[24,128]{1,0:T(8,128)} %bitcast.11, s32[24,128]{1,0:T(8,128)} %bitcast.12, s32[24,128]{1,0:T(8,128)} %bitcast.13, bf16[24,128]{1,0:T(8,128)(2,1)} %bitcast.14, s32[8,128]{1,0:T(8,128)} %bitcast.15, s32[276]{0:T(512)} %sup_in.1, s32[1,11]{1,0:T(1,128)} %bitcast.16), custom_call_target="tpu_custom_call" | custom-call | tf_op jit(solution)/shard_map/revenue/pallas_call | solution.py:251
  22.1 0.0 copy-start
  22.1 1.3 %slice_bitcast_fusion.1 = f32[1024]{0:T(1024)} fusion(f32[24,128]{1,0:T(8,128)} %get-tuple-element.5), kind=kLoop, calls=%fused_computation.1 | loop fusion | bytes 8192 | tf_op jit(solution)/shard_map/reshape | solution.py:297
  23.5 0.0 copy-done
  23.5 0.6 %slice_bitcast_fusion = f32[2048]{0:T(1024)} fusion(f32[24,128]{1,0:T(8,128)S(1)} %copy-done), kind=kLoop, calls=%fused_computation | loop fusion | bytes 16384 | tf_op jit(solution)/shard_map/reshape | solution.py:296
Async XLA Ops:
  22.1 1.4 %copy-start = (f32[24,128]{1,0:T(8,128)S(1)}, f32[24,128]{1,0:T(8,128)}, u32[]{:S(2)}) copy-start(f32[24,128]{1,0:T(8,128)} %get-tuple-element.5) | copy-start | bytes 36868

commit v3 on v2

--- a/solution.py
+++ b/solution.py
@@ -29,9 +29,10 @@
     block_in, offset_in, date_in, rev_in, cand_in, sup_in, dat_in,
     both_ref, total_ref,
     block_ref, offset_ref, date_ref, rev_ref, cand_ref, load_sem, dat_row,
-    a_idx, b_idx, left, right, hist, dat_buf, sup_buf, part1, sum1, part2,
+    ids, rev32, a_idx, b_idx, left, right, low_left, c_hot, dat_buf, sup_buf,
+    peer_ids, peer_dates, peer_revs, sum1, part2,
     cpart, cpart1, csum1, cpart2,
-    dat_send, dat_recv, sup_send, sup_recv, h1_send, h1_recv, c1_send, c1_recv,
+    dat_send, dat_recv, sup_send, sup_recv, row_send, row_recv, c1_send, c1_recv,
     h2_send, h2_recv, c2_send, c2_recv,
 ):
     R, C = rows_axis, cols_axis
@@ -42,7 +43,7 @@
     n_dates, n_words = dat_in.shape[1], sup_in.shape[0]
     per_block = n_words // R
     owned_rows = both_ref.shape[0] - cand_ref.shape[0]
-    chunks = hist.shape[0] // left.shape[0]
+    chunks = R * C * GROUP // left.shape[0]
     tall = left.shape[0]
 
     barrier = pltpu.get_barrier_semaphore()
@@ -61,6 +62,9 @@
         load.wait()
 
     off = offset_ref[...]
+    rev = rev_ref[...].astype(jnp.float32)
+    ids[...] = block_ref[...] * SUP_DEV + off
+    rev32[...] = rev
     a_idx[...] = block_ref[...] * GROUP + (lax.shift_right_logical(off, 7) & (GROUP - 1))
     b_idx[...] = lax.shift_right_logical(off, 10) * LANES + (off & (LANES - 1))
 
@@ -79,79 +83,90 @@
     ]
     for copy in dat_copies:
         copy.start()
+    row_copies = [
+        [
+            remote(src, dst.at[k], row_send.at[n, k], row_recv.at[n, k], row_peers[k])
+            for n, (src, dst) in enumerate(((ids, peer_ids), (date_ref, peer_dates), (rev32, peer_revs)))
+        ]
+        for k in range(R - 1)
+    ]
+    for copies in row_copies:
+        for copy in copies:
+            copy.start()
     for copy in sup_copies:
         copy.start()
 
     iota_b = lax.broadcasted_iota(jnp.int32, (WIDE, LANES), 0)
-    for r in range(n_rows):
-        hit = iota_b == b_idx[r : r + 1, :]
-        right[:, r * LANES : (r + 1) * LANES] = jnp.where(hit, 1.0, 0.0).astype(jnp.bfloat16)
-
-    iota_a = lax.broadcasted_iota(jnp.int32, (tall, LANES), 0)
-    rev = rev_ref[...].astype(jnp.float32)
-
-    def build_left(base, values):
+
+    def build_right(columns):
         for r in range(n_rows):
-            hit = iota_a == a_idx[r : r + 1, :] - base
-            left[:, r * LANES : (r + 1) * LANES] = jnp.where(hit, values[r : r + 1, :], 0.0).astype(jnp.bfloat16)
-
-    day = date_ref[...]
-    day_word = div_bits(day)
-    day_bit = day - day_word * BITS
+            hit = iota_b == columns[r : r + 1, :]
+            right[:, r * LANES : (r + 1) * LANES] = jnp.where(hit, 1.0, 0.0).astype(jnp.bfloat16)
+
+    def build_left(where, lines, values):
+        iota_a = lax.broadcasted_iota(jnp.int32, (where.shape[0], LANES), 0)
+        for r in range(n_rows):
+            hit = iota_a == lines[r : r + 1, :]
+            where[:, r * LANES : (r + 1) * LANES] = jnp.where(hit, values[r : r + 1, :], 0.0).astype(jnp.bfloat16)
+
+    def product(lines, columns):
+        return lax.dot_general(lines, columns, (((1,), (1,)), ((), ())), preferred_element_type=jnp.float32)
+
+    cand = cand_ref[...]
+    c_owner = lax.shift_right_logical(cand, 11)
+    c_off = cand & (SUP_DEV - 1)
+    c_row = c_owner * GROUP + (lax.shift_right_logical(c_off, 7) & (GROUP - 1))
+    c_col = lax.shift_right_logical(c_off, 10) * LANES + (c_off & (LANES - 1))
+    groups = cand.shape[0]
+
+    def build_hot(base):
+        iota_c = lax.broadcasted_iota(jnp.int32, (tall, LANES), 0)
+        for g in range(groups):
+            hit = iota_c == c_row[g : g + 1, :] - base
+            c_hot[:, g * LANES : (g + 1) * LANES] = jnp.where(hit, 1.0, 0.0).astype(jnp.bfloat16)
+
+    if chunks == 1:
+        build_hot(0)
+
+    build_right(b_idx[...])
 
     for copy in dat_copies:
         copy.wait_recv()
     for c in range(C):
         dat_row[:, c * n_dates : (c + 1) * n_dates] = dat_buf[c]
     table = dat_row[...]
-    lit = lax.shift_right_logical(lookup(table, day_word), day_bit) & 1
-    values = jnp.where(lit == 1, rev, 0.0)
-
-    def histogram(base):
-        build_left(base, values)
-        return lax.dot_general(
-            left[...], right[...], (((1,), (1,)), ((), ())), preferred_element_type=jnp.float32
-        )
+
+    def dated(day, values):
+        day_word = div_bits(day)
+        lit = lax.shift_right_logical(lookup(table, day_word), day - day_word * BITS) & 1
+        return jnp.where(lit == 1, values, 0.0)
+
+    values = dated(date_ref[...], rev)
+
+    def candidate_columns(base):
+        build_left(left, a_idx[...] - base, values)
+        rest = product(right[...], left[...])
+        found = jnp.zeros((WIDE, groups * LANES), jnp.float32)
+        for _ in range(3):
+            term = rest.astype(jnp.bfloat16)
+            rest = rest - term.astype(jnp.float32)
+            found = found + jnp.dot(term, c_hot[...], preferred_element_type=jnp.float32)
+        return found
 
     if chunks == 1:
-        hist[...] = histogram(0)
+        found = candidate_columns(0)
     else:
 
-        def body(c, carry):
-            base = pl.multiple_of(c * tall, tall)
-            hist[pl.ds(base, tall), :] = histogram(base)
-            return carry
-
-        lax.fori_loop(0, chunks, body, 0)
-
-    span = C * GROUP
-    h1_copies = [
-        remote(
-            hist.at[pl.ds(pl.multiple_of(row_peers[k][0] * span, span), span), :],
-            part1.at[k], h1_send.at[k], h1_recv.at[k], row_peers[k],
-        )
-        for k in range(R - 1)
-    ]
-    for copy in h1_copies:
-        copy.start()
-
-    cand = cand_ref[...]
-    c_off = cand & (SUP_DEV - 1)
-    c_owner = lax.div(cand, SUP_DEV) if SUP_DEV & (SUP_DEV - 1) else lax.shift_right_logical(cand, 11)
-    c_row = c_owner * GROUP + (lax.shift_right_logical(c_off, 7) & (GROUP - 1))
-    c_high = c_off >= SUP_DEV // 2
-    c_lane = c_off & (LANES - 1)
-
-    def pick(g, acc):
-        base = pl.multiple_of(g * 8, 8)
-        tile = hist[pl.ds(base, 8), :]
-        for s in range(8):
-            low = lookup(tile[s : s + 1, :LANES], c_lane)
-            high = lookup(tile[s : s + 1, LANES:], c_lane)
-            acc = jnp.where(c_row == base + s, jnp.where(c_high, high, low), acc)
-        return acc
-
-    picked = lax.fori_loop(0, hist.shape[0] // 8, pick, jnp.zeros(cand.shape, jnp.float32))
+        def body(c, acc):
+            build_hot(c * tall)
+            return acc + candidate_columns(c * tall)
+
+        found = lax.fori_loop(0, chunks, body, jnp.zeros((WIDE, groups * LANES), jnp.float32))
+    picked = []
+    for g in range(groups):
+        hit = iota_b == c_col[g : g + 1, :]
+        picked.append(jnp.sum(jnp.where(hit, found[:, g * LANES : (g + 1) * LANES], 0.0), axis=0, keepdims=True))
+    picked = jnp.concatenate(picked, axis=0)
     cpart[...] = picked
     cpart1[i] = picked
     c1_copies = [
@@ -160,41 +175,17 @@
     for copy in c1_copies:
         copy.start()
 
-    for copy in sup_copies:
-        copy.wait_recv()
-
-    full = n_words // LANES
-
-    def words_at(source, flat):
-        word = lookup(sup_buf[source, :, n_words - LANES :], jnp.maximum(flat - (n_words - LANES), 0))
-        for t in range(full):
-            near = (flat >= t * LANES) & (flat < (t + 1) * LANES)
-            word = jnp.where(near, lookup(sup_buf[source, :, t * LANES : (t + 1) * LANES], flat & (LANES - 1)), word)
-        return word
-
-    c_word = div_bits(c_off)
-    c_bit = c_off - c_word * BITS
-    c_col = lax.div(c_owner, R)
-    c_flat = (c_owner - c_col * R) * per_block + c_word
-
-    def word_of(source, acc):
-        return jnp.where(c_col == source, words_at(source, c_flat), acc)
-
-    c_words = lax.fori_loop(0, C, word_of, jnp.zeros(cand.shape, jnp.int32))
-    c_lit = (lax.shift_right_logical(c_words, c_bit) & 1) == 1
-
-    me = i * C + j
-    shape = (owned_rows, LANES)
-    spot = lax.broadcasted_iota(jnp.int32, shape, 0) * LANES + lax.broadcasted_iota(jnp.int32, shape, 1)
-    spot_word = div_bits(spot)
-    my_words = words_at(me // R, lax.rem(me, R) * per_block + spot_word)
-    my_lit = (lax.shift_right_logical(my_words, spot - spot_word * BITS) & 1) == 1
-
-    for copy in h1_copies:
-        copy.wait_recv()
-    total = hist[pl.ds(pl.multiple_of(i * span, span), span), :]
+    span = C * GROUP
+    build_left(low_left, a_idx[...] - i * span, values)
+    total = product(low_left[...], right[...])
     for k in range(R - 1):
-        total = total + part1[k]
+        for copy in row_copies[k]:
+            copy.wait_recv()
+        peer_id = peer_ids[k]
+        line = lax.shift_right_logical(peer_id, 11) * GROUP + (lax.shift_right_logical(peer_id, 7) & (GROUP - 1))
+        build_right((lax.shift_right_logical(peer_id, 10) & 1) * LANES + (peer_id & (LANES - 1)))
+        build_left(low_left, line - i * span, dated(peer_dates[k], peer_revs[k]))
+        total = total + product(low_left[...], right[...])
     sum1[...] = total
     h2_copies = [
         remote(
@@ -205,6 +196,7 @@
     ]
     for copy in h2_copies:
         copy.start()
+
     for copy in c1_copies:
         copy.wait_recv()
     ctotal = cpart1[0]
@@ -218,6 +210,36 @@
     for copy in c2_copies:
         copy.start()
 
+    for copy in sup_copies:
+        copy.wait_recv()
+
+    full = n_words // LANES
+
+    def words_at(source, flat):
+        word = lookup(sup_buf[source, :, n_words - LANES :], jnp.maximum(flat - (n_words - LANES), 0))
+        for t in range(full):
+            near = (flat >= t * LANES) & (flat < (t + 1) * LANES)
+            word = jnp.where(near, lookup(sup_buf[source, :, t * LANES : (t + 1) * LANES], flat & (LANES - 1)), word)
+        return word
+
+    c_word = div_bits(c_off)
+    c_bit = c_off - c_word * BITS
+    c_source = lax.div(c_owner, R)
+    c_flat = (c_owner - c_source * R) * per_block + c_word
+
+    def word_of(source, acc):
+        return jnp.where(c_source == source, words_at(source, c_flat), acc)
+
+    c_words = lax.fori_loop(0, C, word_of, jnp.zeros(cand.shape, jnp.int32))
+    c_lit = (lax.shift_right_logical(c_words, c_bit) & 1) == 1
+
+    me = i * C + j
+    shape = (owned_rows, LANES)
+    spot = lax.broadcasted_iota(jnp.int32, shape, 0) * LANES + lax.broadcasted_iota(jnp.int32, shape, 1)
+    spot_word = div_bits(spot)
+    my_words = words_at(me // R, lax.rem(me, R) * per_block + spot_word)
+    my_lit = (lax.shift_right_logical(my_words, spot - spot_word * BITS) & 1) == 1
+
     for copy in h2_copies:
         copy.wait_recv()
     mine = sum1[pl.ds(pl.multiple_of(j * GROUP, GROUP), GROUP), :]
@@ -235,7 +257,7 @@
     both_ref[owned_rows:, :] = result
     total_ref[0, 0] = jnp.sum(result)
 
-    for copy in dat_copies + sup_copies + h1_copies + c1_copies + h2_copies + c2_copies:
+    for copy in dat_copies + sup_copies + sum(row_copies, []) + c1_copies + h2_copies + c2_copies:
         copy.wait_send()
 
 
@@ -265,13 +287,18 @@
             dma((7,)),
             pltpu.VMEM((1, LANES), i32),
             pltpu.VMEM((rows, LANES), i32),
+            pltpu.VMEM((rows, LANES), f32),
+            pltpu.VMEM((rows, LANES), i32),
             pltpu.VMEM((rows, LANES), i32),
             pltpu.VMEM((tall, rows * LANES), jnp.bfloat16),
             pltpu.VMEM((WIDE, rows * LANES), jnp.bfloat16),
-            pltpu.VMEM((tall_all, WIDE), f32),
+            pltpu.VMEM((span, rows * LANES), jnp.bfloat16),
+            pltpu.VMEM((tall, cands * LANES), jnp.bfloat16),
             pltpu.VMEM((C, 1, date_words.shape[0]), i32),
             pltpu.VMEM((C, 1, supplier_words.shape[0]), i32),
-            pltpu.VMEM((R - 1, span, WIDE), f32),
+            pltpu.VMEM((R - 1, rows, LANES), i32),
+            pltpu.VMEM((R - 1, rows, LANES), i32),
+            pltpu.VMEM((R - 1, rows, LANES), f32),
             pltpu.VMEM((span, WIDE), f32),
             pltpu.VMEM((C - 1, GROUP, WIDE), f32),
             pltpu.VMEM((cands, LANES), f32),
@@ -279,7 +306,7 @@
             pltpu.VMEM((cands, LANES), f32),
             pltpu.VMEM((C, cands, LANES), f32),
             dma((C - 1,)), dma((C - 1,)), dma((C - 1,)), dma((C - 1,)),
-            dma((R - 1,)), dma((R - 1,)), dma((R - 1,)), dma((R - 1,)),
+            dma((3, R - 1)), dma((3, R - 1)), dma((R - 1,)), dma((R - 1,)),
             dma((C - 1,)), dma((C - 1,)), dma((C - 1,)), dma((C - 1,)),
         ],
         compiler_params=pltpu.CompilerParams(collective_id=0, has_side_effects=True),

time: 26.1 us -> 24.7 us (0.946)
  Pallas kernels: 21.5 us -> 20.1 us
    pallas_call x1, Pallas kernels: 21.5 us -> 20.1 us  [per_device(): pl.pallas_call(functools.partial(kernel, R, C), out_shape=(jax.ShapeDtype...]
where the time goes in v3:
time: 24.7 us; the launch traced here: 24.4 us
  Pallas kernels  20.1 us (81%)
  between operations  2.41 us (10%)
  local copies, waits for them, and re-layouts  1.94 us (8%)
    pallas_call x1, Pallas kernels, per_device(): pl.pallas_call(functools.partial(kernel, R, C), out_shape=(jax.ShapeDtype...  20.1 us
    reshape x1, local copies, waits for them, and re-layouts, per_device(): both[SUP_DEV // LANES:].reshape(candidates.shape)  1.34 us
    reshape x1, local copies, waits for them, and re-layouts, per_device(): owned = both[:SUP_DEV // LANES].reshape(SUP_DEV)  0.6 us

profile of v3, /device:TPU:0, one launch (start us, length us, event | category | flops | bytes accessed | tf_op | source)
XLA Modules:
  0.0 24.4 jit_solution(4150649003367137587)
XLA Ops:
  0.6 20.1 %revenue.1 = (f32[24,128]{1,0:T(8,128)}, f32[1,1]{1,0:T(1,128)}) custom-call(s32[24,128]{1,0:T(8,128)} %bitcast.11, s32[24,128]{1,0:T(8,128)} %bitcast.12, s32[24,128]{1,0:T(8,128)} %bitcast.13, bf16[24,128]{1,0:T(8,128)(2,1)} %bitcast.14, s32[8,128]{1,0:T(8,128)} %bitcast.15, s32[276]{0:T(512)} %sup_in.1, s32[1,11]{1,0:T(1,128)} %bitcast.16), custom_call_target="tpu_custom_call" | custom-call | tf_op jit(solution)/shard_map/revenue/pallas_call | solution.py:273
  20.7 0.0 copy-start
  20.7 1.3 %slice_bitcast_fusion.1 = f32[1024]{0:T(1024)} fusion(f32[24,128]{1,0:T(8,128)} %get-tuple-element.5), kind=kLoop, calls=%fused_computation.1 | loop fusion | bytes 8192 | tf_op jit(solution)/shard_map/reshape | solution.py:324
  22.1 0.0 copy-done
  22.1 0.6 %slice_bitcast_fusion = f32[2048]{0:T(1024)} fusion(f32[24,128]{1,0:T(8,128)S(1)} %copy-done), kind=kLoop, calls=%fused_computation | loop fusion | bytes 16384 | tf_op jit(solution)/shard_map/reshape | solution.py:323
Async XLA Ops:
  20.7 1.4 %copy-start = (f32[24,128]{1,0:T(8,128)S(1)}, f32[24,128]{1,0:T(8,128)}, u32[]{:S(2)}) copy-start(f32[24,128]{1,0:T(8,128)} %get-tuple-element.5) | copy-start | bytes 36868

commit v4 on v3

--- a/solution.py
+++ b/solution.py
@@ -27,7 +27,7 @@
 def kernel(
     rows_axis, cols_axis,
     block_in, offset_in, date_in, rev_in, cand_in, sup_in, dat_in,
-    both_ref, total_ref,
+    both_ref,
     block_ref, offset_ref, date_ref, rev_ref, cand_ref, load_sem, dat_row,
     ids, rev32, a_idx, b_idx, left, right, low_left, c_hot, dat_buf, sup_buf,
     peer_ids, peer_dates, peer_revs, sum1, part2,
@@ -127,6 +127,7 @@
 
     if chunks == 1:
         build_hot(0)
+        build_left(left, a_idx[...], rev)
 
     build_right(b_idx[...])
 
@@ -141,10 +142,15 @@
         lit = lax.shift_right_logical(lookup(table, day_word), day - day_word * BITS) & 1
         return jnp.where(lit == 1, values, 0.0)
 
-    values = dated(date_ref[...], rev)
+    lit_rows = dated(date_ref[...], jnp.ones_like(rev))
+    for r in range(n_rows):
+        part = right[:, r * LANES : (r + 1) * LANES]
+        shown = jnp.broadcast_to(lit_rows[r : r + 1, :], part.shape).astype(jnp.bfloat16)
+        right[:, r * LANES : (r + 1) * LANES] = part * shown
 
     def candidate_columns(base):
-        build_left(left, a_idx[...] - base, values)
+        if chunks > 1:
+            build_left(left, a_idx[...] - base, rev)
         rest = product(right[...], left[...])
         found = jnp.zeros((WIDE, groups * LANES), jnp.float32)
         for _ in range(3):
@@ -176,8 +182,11 @@
         copy.start()
 
     span = C * GROUP
-    build_left(low_left, a_idx[...] - i * span, values)
-    total = product(low_left[...], right[...])
+    if chunks == 1:
+        total = product(left[pl.ds(pl.multiple_of(i * span, span), span), :], right[...])
+    else:
+        build_left(low_left, a_idx[...] - i * span, rev)
+        total = product(low_left[...], right[...])
     for k in range(R - 1):
         for copy in row_copies[k]:
             copy.wait_recv()
@@ -255,10 +264,17 @@
         ctotal = ctotal + cpart2[k]
     result = jnp.where(c_lit, ctotal, 0.0)
     both_ref[owned_rows:, :] = result
-    total_ref[0, 0] = jnp.sum(result)
 
     for copy in dat_copies + sup_copies + sum(row_copies, []) + c1_copies + h2_copies + c2_copies:
         copy.wait_send()
+
+
+def finish(both_ref, owned_ref, cand_out_ref, total_ref):
+    owned_rows = owned_ref.shape[0]
+    owned_ref[...] = both_ref[:owned_rows, :]
+    found = both_ref[owned_rows:, :]
+    cand_out_ref[...] = found
+    total_ref[0, 0] = jnp.sum(found)
 
 
 def per_device(R, C, fact_block, fact_offset, fact_date, revenue, supplier_words, date_words, candidates):
@@ -270,14 +286,11 @@
     f32, i32 = jnp.float32, jnp.int32
     dma = pltpu.SemaphoreType.DMA
     vmem = pl.BlockSpec(memory_space=pltpu.VMEM)
-    both, total = pl.pallas_call(
+    both = pl.pallas_call(
         functools.partial(kernel, R, C),
-        out_shape=(
-            jax.ShapeDtypeStruct((SUP_DEV // LANES + cands, LANES), f32),
-            jax.ShapeDtypeStruct((1, 1), f32),
-        ),
+        out_shape=jax.ShapeDtypeStruct((SUP_DEV // LANES + cands, LANES), f32),
         in_specs=[pl.BlockSpec(memory_space=pl.ANY)] * 7,
-        out_specs=(vmem, pl.BlockSpec(memory_space=pltpu.SMEM)),
+        out_specs=vmem,
         scratch_shapes=[
             pltpu.VMEM((rows, LANES), i32),
             pltpu.VMEM((rows, LANES), i32),
@@ -320,8 +333,18 @@
         supplier_words,
         date_words.reshape(1, -1),
     )
-    owned = both[: SUP_DEV // LANES].reshape(SUP_DEV)
-    return owned, both[SUP_DEV // LANES :].reshape(candidates.shape), total.reshape(())
+    owned, found, total = pl.pallas_call(
+        finish,
+        out_shape=(
+            jax.ShapeDtypeStruct((SUP_DEV // LANES, LANES), f32),
+            jax.ShapeDtypeStruct((cands, LANES), f32),
+            jax.ShapeDtypeStruct((1, 1), f32),
+        ),
+        in_specs=[vmem],
+        out_specs=(vmem, vmem, pl.BlockSpec(memory_space=pltpu.SMEM)),
+        name="finish",
+    )(both)
+    return owned.reshape(SUP_DEV), found.reshape(candidates.shape), total.reshape(())
 
 
 def solution(mesh):

time: 24.7 us -> 22.3 us (0.903)
  local copies, waits for them, and re-layouts: 1.94 us -> 0 us
  between operations: 2.41 us -> 0.64 us
  Pallas kernels: 20.1 us -> 21.3 us
    reshape x2 -> x0, local copies, waits for them, and re-layouts: 1.94 us -> none  [the longest x1 1.34 us: per_device(): both[SUP_DEV // LANES:].reshape(candidates.shape)]
    pallas_call x1 -> x2, Pallas kernels: 20.1 us -> 21.3 us  [the longest x1 19.9 us: per_device(): pl.pallas_call(functools.partial(kernel, R, C), out_shape=jax.ShapeDtypeS...]
where the time goes in v4:
time: 22.3 us; the launch traced here: 21.9 us
  Pallas kernels  21.3 us (96%)
  between operations  0.64 us (3%)
    pallas_call x1, Pallas kernels, per_device(): pl.pallas_call(functools.partial(kernel, R, C), out_shape=jax.ShapeDtypeS...  19.9 us
    pallas_call x1, Pallas kernels, per_device(): pl.pallas_call(finish, out_shape=(jax.ShapeDtypeStruct((SUP_DEV // LANES,...  1.34 us

profile of v4, /device:TPU:0, one launch (start us, length us, event | category | flops | bytes accessed | tf_op | source)
XLA Modules:
  0.0 21.9 jit_solution(899977320725673409)
XLA Ops:
  0.6 19.9 %revenue.1.both_ref = f32[24,128]{1,0:T(8,128)} custom-call(s32[24,128]{1,0:T(8,128)} %bitcast.9, s32[24,128]{1,0:T(8,128)} %bitcast.10, s32[24,128]{1,0:T(8,128)} %bitcast.11, bf16[24,128]{1,0:T(8,128)(2,1)} %bitcast.12, s32[8,128]{1,0:T(8,128)} %bitcast.13, s32[276]{0:T(512)} %sup_in.1, s32[1,11]{1,0:T(1,128)} %bitcast.14), custom_call_target="tpu_custom_call" | custom-call | tf_op jit(solution)/shard_map/revenue/pallas_call | solution.py:289
  20.6 1.3 %finish.1 = (f32[16,128]{1,0:T(8,128)}, f32[8,128]{1,0:T(8,128)}, f32[1,1]{1,0:T(1,128)}) custom-call(f32[24,128]{1,0:T(8,128)} %revenue.1.both_ref), custom_call_target="tpu_custom_call" | custom-call | tf_op jit(solution)/shard_map/finish/pallas_call | solution.py:336
